TPU v7x, 32 devices: a whole 2x2x4 slice. The times are simulated.
32 devices in a mesh: grp: 2 (over y), section: 2 (over core), seq: 4 (over z), fsdp: 2 (over x).
Axes of the slice: x: 2, y: 2, z: 4, core: 2. Of those that a mesh axis runs over, the one named last changes fastest.
Arguments:
- head_inputs: bfloat16 [2, 4, 256, 7680], P('section', ('grp', 'fsdp'), 'seq'), parts along dimension 1, may hold values from -8 to 8
- hidden: bfloat16 [2, 4, 256, 2560], P('section', ('grp', 'fsdp'), 'seq'), parts along dimension 1, may hold values from -3 to 3
- out_weight: bfloat16 [2, 2560, 2560], P('section', 'fsdp'), may hold values from -0.125 to 0.125
- time_weight: bfloat16 [2, 256, 7680], P('section', None, ('seq', 'fsdp')), may hold values from -0.375 to 0.375
- head_weight: bfloat16 [2, 2560, 64], P('section', ('seq', 'fsdp')), may hold values from -0.125 to 0.125
- latent: float32 [2, 4, 128, 128], P('section', ('grp', 'fsdp'), 'seq'), parts along dimension 1, may hold values from -6 to 6
- timesteps: int32 [2, 4, 2], P('section', ('grp', 'fsdp')), parts along dimension 1, may hold values from 41 to 999, as said below
Outputs:
- velocity: float32 [2, 4, 128, 128], P('section', ('grp', 'fsdp'), 'seq'), parts along dimension 1
- carried: float32 [2, 4, 128, 128], P('section', ('grp', 'fsdp'), 'seq'), parts along dimension 1
There are 2 independent parts, one for each index of `grp`. A program takes and returns all parts, laid end to end along the dimension named above; an argument that names none is the same for every part. Nothing has to cross between parts.
Inputs may be any that keep to these rules, and one draw needn't show every extreme that they name: timesteps[0] lie in 875 to 999 and timesteps[1] in 100 to 874 for the current entry; the next entry is the current one minus 10 to 59.
All inputs are finite; a program needn't handle non-finite values.
Results may differ from a plain program's by a relative error of at most 0.0049.
Values may be sent and summed in bfloat16 or wider, within the bound.
No kernel may reach another device: no remote copies, remote signals or barrier semaphores. Data moves between devices by JAX's collectives and lax.ppermute only.
A program may use at most 128 MiB of HBM per device.

v0:
```python
import math
import jax
import jax.numpy as jnp
from jax import lax
from jax.sharding import PartitionSpec as P

DIM = 2560
HEADS = 32
HEAD = 80
PATCH = 64
FREQ = 256


def partner(block, axis, apart):
    count = lax.axis_size(axis)
    route = []
    for low in range(count):
        high = low | 1 << apart
        if high != low and high < count:
            route += [(low, high), (high, low)]
    return lax.ppermute(block, axis, route)


def time_embed(steps_now):
    half = FREQ // 2
    freqs = jnp.exp(-math.log(10000.0) * jnp.arange(half, dtype=jnp.float32) / half)
    angle = steps_now.astype(jnp.float32)[..., None] * freqs
    return jnp.concatenate([jnp.cos(angle), jnp.sin(angle)], axis=-1)


def sigma_of(steps_now):
    unit_time = steps_now.astype(jnp.float32) / 1000.0
    return 5.0 * unit_time / (1.0 + 4.0 * unit_time)


def attend(exchanged):
    items = exchanged.shape[0]
    length = exchanged.shape[1]
    local_heads = exchanged.shape[2]
    query_all = exchanged[..., :HEAD]
    key_rows = exchanged[..., HEAD : 2 * HEAD]
    value_rows = exchanged[..., 2 * HEAD :]
    block_rows = min(512, length)
    block_count = length // block_rows

    def one_block(block_index):
        query_block = lax.dynamic_slice_in_dim(query_all, block_index * block_rows, block_rows, 1)
        scores = jnp.einsum(
            "nqhe,nkhe->nhqk", query_block, key_rows, preferred_element_type=jnp.float32
        ) * HEAD ** (-0.5)
        row_max = jnp.max(scores, axis=-1, keepdims=True)
        exp_scores = jnp.exp(scores - row_max)
        row_sum = jnp.sum(exp_scores, axis=-1, keepdims=True)
        weights = (exp_scores / row_sum).astype(jnp.bfloat16)
        return jnp.einsum(
            "nhqk,nkhe->nqhe", weights, value_rows, preferred_element_type=jnp.float32
        ).astype(jnp.bfloat16)

    blocks = lax.map(one_block, jnp.arange(block_count, dtype=jnp.int32))
    return blocks.transpose(1, 0, 2, 3, 4).reshape(items, length, local_heads * HEAD)


def body(head_inputs, hidden, out_weight, time_weight, head_weight, latent, timesteps):
    samples = head_inputs.shape[1]
    row_count = head_inputs.shape[2]
    flat_count = samples * row_count
    local = head_inputs.reshape(samples, row_count, HEADS, 3 * HEAD)
    attended = lax.all_to_all(
        attend(lax.all_to_all(local, "seq", split_axis=2, concat_axis=1, tiled=True)),
        "seq",
        split_axis=1,
        concat_axis=2,
        tiled=True,
    )
    flattened = attended.reshape(flat_count, HEADS * HEAD)
    time_full, head_full = (
        lax.all_gather(time_weight, ("seq", "fsdp"), axis=2, tiled=True),
        lax.all_gather(head_weight, ("seq", "fsdp"), axis=1, tiled=True),
    )
    embedding = time_embed(timesteps[0, :, 0]).astype(jnp.bfloat16)
    modulation = jnp.dot(embedding, time_full[0], preferred_element_type=jnp.float32)
    gate_term = modulation[:, None, :DIM]
    shift_term = modulation[:, None, DIM : 2 * DIM]
    scale_term = modulation[:, None, 2 * DIM :]
    own_columns = lax.all_to_all(flattened, "fsdp", split_axis=1, concat_axis=0, tiled=True)
    projected = lax.psum_scatter(
        jnp.dot(own_columns, out_weight[0], preferred_element_type=jnp.float32).astype(
            jnp.bfloat16
        ),
        "fsdp",
        scatter_dimension=0,
        tiled=True,
    ).astype(jnp.float32)
    updated = hidden.reshape(samples, row_count, DIM).astype(
        jnp.float32
    ) + gate_term * projected.reshape(samples, row_count, DIM)
    average = jnp.mean(updated, axis=-1, keepdims=True)
    centred = updated - average
    variance = jnp.mean(centred * centred, axis=-1, keepdims=True)
    normed = (centred * lax.rsqrt(variance + 1e-06) * (1.0 + scale_term) + shift_term).astype(
        jnp.bfloat16
    )
    velocity = jnp.dot(
        normed.reshape(flat_count, DIM), head_full[0], preferred_element_type=jnp.float32
    )
    velocity = velocity.reshape(1, samples, row_count // 2, 2 * PATCH)
    step_size = sigma_of(timesteps[0, :, 1]) - sigma_of(timesteps[0, :, 0])
    stepped = latent + step_size[None, :, None, None] * velocity
    carried = partner(stepped, "section", 0)
    return (velocity, carried)


def solution(mesh):
    return jax.shard_map(
        body,
        mesh=mesh,
        in_specs=(
            P("section", ("grp", "fsdp"), "seq", None),
            P("section", ("grp", "fsdp"), "seq", None),
            P("section", "fsdp", None),
            P("section", None, ("seq", "fsdp")),
            P("section", ("seq", "fsdp"), None),
            P("section", ("grp", "fsdp"), "seq", None),
            P("section", ("grp", "fsdp"), None),
        ),
        out_specs=(
            P("section", ("grp", "fsdp"), "seq", None),
            P("section", ("grp", "fsdp"), "seq", None),
        ),
        check_vma=False,
    )
```

profile of v0, /device:TPU:0, one launch (start us, length us, event | category | flops | bytes accessed | tf_op | source)
XLA Modules:
  0.0 163.8 jit_solution(13938546322388415020)
XLA Ops:
  8.0 0.0 all-gather.2.cloned.1.call-start
  8.0 0.7 all-gather.2.cloned.1.call-update
  8.7 0.0 reduce-scatter.2.cloned.1.call-start
  8.8 3.5 %reshape.152 = bf16[1,64,32,240]{3,2,1,0:T(8,128)(2,1)S(1)} reshape(bf16[1,1,64,7680]{3,2,1,0:T(8,128)(2,1)} %param.7) | data formatting | bytes 1966080 | tf_op jit(solution)/shard_map/reshape | solution.py:67
  12.3 0.6 copy.28
  12.9 47.7 %all_to_all.52 = bf16[1,64,32,240]{3,1,0,2:T(8,128)(2,1)S(1)} all-to-all(bf16[1,64,32,240]{3,1,0,2:T(8,128)(2,1)S(1)} %copy.28), channel_id=1, replica_groups=mesh['grp'=2,'section'=2,'seq'=4,'fsdp'=2] {'seq'}, dimensions={2} | all-to-all | bytes 1966080 | tf_op jit(solution)/shard_map/all_to_all | solution.py:69
  60.6 0.6 copy.46
  61.2 0.1 copy.30
  61.2 0.4 fusion.35
  61.7 0.3 copy.42
  62.0 0.3 copy.43
  62.3 0.3 copy.44
  62.7 2.2 %fusion.37 = (f32[8,256]{1,0:T(8,128)S(1)}, f32[8,256,256]{1,2,0:T(8,128)}) fusion(bf16[1,256,8,80]{1,3,2,0:T(8,128)(2,1)S(1)} %copy.44, bf16[1,256,8,80]{1,3,2,0:T(8,128)(2,1)S(1)} %copy.43), kind=kOutput, calls=%fused_computation.41 | convolution fusion | flops 85459200 | bytes 2760704 | tf_op jit(solution)/shard_map/while/body/eval_jaxpr/sub | solution.py:52
  64.8 1.9 %convolution_convert_fusion = bf16[8,256,80]{1,2,0:T(8,128)(2,1)S(1)} fusion(f32[8,256,256]{1,2,0:T(8,128)} %get-tuple-element.26, f32[8,256]{1,0:T(8,128)S(1)} %get-tuple-element.25, bf16[1,256,8,80]{1,3,2,0:T(8,128)(2,1)S(1)} %copy.42), kind=kOutput, calls=%fused_computation.10 | convolution fusion | flops 85098496 | bytes 2760704 | tf_op jit(solution)/shard_map/while/body/eval_jaxpr/nhqk,nkhe->nqhe/dot_general | solution.py:55
  66.7 0.6 copy.35
  67.3 0.5 broadcast.88
  67.9 2.6 %reduce.14 = bf16[256,640]{1,0:T(8,128)(2,1)S(1)} reduce(bf16[256,1,640]{2,1,0:T(2,128)(2,1)S(1)} %bitcast.71, bf16[]{:T(256)} %broadcast.88), dimensions={1}, to_apply=%bitcast.60.reduce_sub_computation | reduce | bytes 655362
  70.5 0.1 reshape.166
  70.6 22.7 %all_to_all.53 = bf16[4,2,20480]{2,1,0:T(2,128)(2,1)S(1)} all-to-all(bf16[4,2,20480]{2,1,0:T(2,128)(2,1)S(1)} %reshape.166), channel_id=1, replica_groups=mesh['grp'=2,'section'=2,'seq'=4,'fsdp'=2] {'seq'}, dimensions={0} | all-to-all | bytes 655360 | tf_op jit(solution)/shard_map/all_to_all | solution.py:68
  93.2 0.3 reshape.167
  93.6 0.3 copy.36
  93.9 0.2 all_to_all.45
  94.1 8.1 %all_to_all.54 = bf16[64,2,1280]{2,0,1:T(8,128)(2,1)S(1)} all-to-all(bf16[64,2,1280]{2,0,1:T(8,128)(2,1)S(1)} %copy.37), channel_id=1, replica_groups=mesh['grp'=2,'section'=2,'seq'=4,'fsdp'=2] {'fsdp'}, dimensions={1} | all-to-all | bytes 655360 | tf_op jit(solution)/shard_map/all_to_all | solution.py:85
  102.2 0.0 copy-start.4
  102.2 0.0 copy-start.2
  102.2 4.7 %fusion.5 = bf16[128,2560]{1,0:T(8,128)(2,1)} fusion(bf16[128,1280]{1,0:T(8,128)(2,1)S(1)} %bitcast.73, bf16[1,1280,2560]{2,1,0:T(8,128)(2,1)} %param.9), kind=kOutput, calls=%fused_computation.5 | convolution fusion | flops 839188480 | bytes 7536640 | tf_op jit(solution)/shard_map/dot_general | solution.py:87
  106.9 0.0 reduce-scatter.2.cloned.1.call-update
  106.9 0.0 copy-done.4
  107.0 0.6 fusion.36
  108.8 0.1 sine_convert_fusion
  108.9 0.0 copy-done.2
  108.9 0.2 copy.38
  109.1 37.3 %all_gather.7 = bf16[1,2560,64]{2,0,1:T(2,128)(2,1)S(1)} all-gather(bf16[1,320,64]{2,0,1:T(2,128)(2,1)S(1)} %copy.38), channel_id=1, replica_groups=mesh['grp'=2,'section'=2,'seq'=4,'fsdp'=2] {'seq','fsdp'}, dimensions={1}, use_global_device_ids=true | all-gather | bytes 368640 | tf_op jit(solution)/shard_map/all_gather | solution.py:78
  146.4 0.8 copy.39
  147.1 0.0 copy-start
  147.2 0.0 all-gather.2.cloned.1.call-done
  147.3 3.2 %fusion.3 = f32[1,7680]{1,0:T(1,128)S(1)} fusion(bf16[256,1]{0,1:T(2,128)(2,1)S(1)} %reshape.160, bf16[1,256,7680]{1,2,0:T(8,128)(2,1)} %all-gather.2.cloned.1.call-done), kind=kOutput, calls=%fused_computation.3 | convolution fusion | flops 3932160 | bytes 3963392 | tf_op jit(solution)/shard_map/dot_general | solution.py:81
  150.5 0.0 copy-start.3
  150.5 0.1 slice_reduce_fusion.1
  150.6 0.0 reduce-scatter.2.cloned.1.call-done
  150.6 0.0 copy-done
  150.6 1.2 fusion.10
  151.8 1.2 multiply_reduce_fusion.1
  153.1 1.3 fusion.11
  154.4 0.1 reshape.156
  154.5 0.0 copy-start.1
  154.5 0.0 copy-done.3
  154.5 0.1 collective-permute-start
  154.6 1.2 collective-permute-done
  155.7 0.6 copy.48
  156.3 0.0 copy-done.1
  (7 shorter events, 0.1 us)
Async XLA Ops:
  8.0 139.3 %all-gather.2.cloned.1.call-start = ((), (), s32[]{:S(2)}) async-start(), calls=%async_computation.4 | async-start | bytes 4423680 | tf_op jit(solution)/shard_map/all_gather | solution.py:77
  8.7 141.9 %reduce-scatter.2.cloned.1.call-start = ((), (), s32[]{:S(2)}) async-start(), calls=%async_computation.5 | async-start | bytes 983040 | tf_op jit(solution)/shard_map/reduce_scatter | solution.py:86
  102.2 4.8 %copy-start.4 = (s32[1,1,2]{2,1,0:T(1,128)S(1)}, s32[1,1,2]{2,1,0:T(1,128)}, u32[]{:S(2)}) copy-start(s32[1,1,2]{2,1,0:T(1,128)} %param.13) | copy-start | bytes 28
  102.2 6.7 %copy-start.2 = (bf16[1,320,64]{1,2,0:T(8,128)(2,1)S(1)}, bf16[1,320,64]{1,2,0:T(8,128)(2,1)}, u32[]{:S(2)}) copy-start(bf16[1,320,64]{1,2,0:T(8,128)(2,1)} %param.11) | copy-start | bytes 122884
  147.1 3.5 %copy-start = (bf16[1,1,64,2560]{3,2,1,0:T(8,128)(2,1)S(1)}, bf16[1,1,64,2560]{3,2,1,0:T(8,128)(2,1)}, u32[]{:S(2)}) copy-start(bf16[1,1,64,2560]{3,2,1,0:T(8,128)(2,1)} %param.8) | copy-start | bytes 983044
  150.5 4.0 %copy-start.3 = (f32[1,1,32,128]{3,2,1,0:T(8,128)S(1)}, f32[1,1,32,128]{3,2,1,0:T(8,128)}, u32[]{:S(2)}) copy-start(f32[1,1,32,128]{3,2,1,0:T(8,128)} %param.12) | copy-start | bytes 49156
  154.5 1.9 %copy-start.1 = (f32[1,1,32,128]{3,2,1,0:T(8,128)}, f32[1,1,32,128]{3,2,1,0:T(8,128)S(1)}, u32[]{:S(2)}) copy-start(f32[1,1,32,128]{3,2,1,0:T(8,128)S(1)} %reshape.156) | copy-start | bytes 49156
  154.5 1.2 collective-permute-start
Sparse Core Ops, SparseCore 0:
  11.0 94.3 all-gather.1
Sparse Core Ops, SparseCore 1:
  107.0 29.8 reduce-scatter.1
where the time goes:
time: 164 us
  blocking collectives  116 us (71%)
  between operations  17.1 us (10%)
  matrix products  13.4 us (8%)
  local copies, waits for them, and re-layouts  10.4 us (6%)
  other arithmetic  5.18 us (3%)
  waiting for transfers between devices  1.92 us (1%)
    all_to_all x1, blocking collectives, body(): lax.all_to_all(local, 'seq', split_axis=2, concat_axis=1, tiled=True)  47.7 us
    all_gather x1, blocking collectives, body(): lax.all_gather(head_weight, ('seq', 'fsdp'), axis=1, tiled=True)  37.3 us
    all_to_all x1, blocking collectives, body(): lax.all_to_all(attend(lax.all_to_all(local, 'seq', split_axis=2, concat_a...  22.7 us
    all_to_all x1, blocking collectives, body(): lax.all_to_all(flattened, 'fsdp', split_axis=1, concat_axis=0, tiled=True)  8.07 us
    dot_general x1, matrix products, body(): jnp.dot(own_columns, out_weight[0], preferred_element_type=jnp.float32)  4.74 us
    reshape x2, local copies, waits for them, and re-layouts, body(): local = head_inputs.reshape(samples, row_count, HEADS, 3 * HEAD)  4.12 us
  transfers between devices with their start and end apart: 3, of which 1 were waited for; matrix products, arithmetic and copies ran while one was open for 15% of the time, Pallas kernels for 0%

commit v1 on v0

--- a/solution.py
+++ b/solution.py
@@ -75,7 +75,7 @@
     flattened = attended.reshape(flat_count, HEADS * HEAD)
     time_full, head_full = (
         lax.all_gather(time_weight, ("seq", "fsdp"), axis=2, tiled=True),
-        lax.all_gather(head_weight, ("seq", "fsdp"), axis=1, tiled=True),
+        jnp.concatenate(lax.all_gather(head_weight, ("seq", "fsdp")), axis=1),
     )
     embedding = time_embed(timesteps[0, :, 0]).astype(jnp.bfloat16)
     modulation = jnp.dot(embedding, time_full[0], preferred_element_type=jnp.float32)

time: 164 us -> 158 us (0.963)
  blocking collectives: 116 us -> 110 us
    all_gather x1, blocking collectives: 37.3 us -> 31.4 us  [body(): lax.all_gather(head_weight, ('seq', 'fsdp'))]
where the time goes in v1:
time: 158 us
  blocking collectives  110 us (70%)
  between operations  17.1 us (11%)
  matrix products  13.4 us (8%)
  local copies, waits for them, and re-layouts  10 us (6%)
  other arithmetic  5.18 us (3%)
  waiting for transfers between devices  1.92 us (1%)
    all_to_all x1, blocking collectives, body(): lax.all_to_all(local, 'seq', split_axis=2, concat_axis=1, tiled=True)  47.7 us
    all_gather x1, blocking collectives, body(): lax.all_gather(head_weight, ('seq', 'fsdp'))  31.4 us
    all_to_all x1, blocking collectives, body(): lax.all_to_all(attend(lax.all_to_all(local, 'seq', split_axis=2, concat_a...  22.7 us
    all_to_all x1, blocking collectives, body(): lax.all_to_all(flattened, 'fsdp', split_axis=1, concat_axis=0, tiled=True)  8.07 us
    dot_general x1, matrix products, body(): jnp.dot(own_columns, out_weight[0], preferred_element_type=jnp.float32)  4.74 us
    reshape x2, local copies, waits for them, and re-layouts, body(): local = head_inputs.reshape(samples, row_count, HEADS, 3 * HEAD)  4.12 us
    dot_general x1, matrix products, body(): jnp.dot(embedding, time_full[0], preferred_element_type=jnp.float32)  3.22 us
  transfers between devices with their start and end apart: 3, of which 1 were waited for; matrix products, arithmetic and copies ran while one was open for 15% of the time, Pallas kernels for 0%

profile of v1, /device:TPU:0, one launch (start us, length us, event | category | flops | bytes accessed | tf_op | source)
XLA Modules:
  0.0 157.5 jit_solution(7981841623644300827)
XLA Ops:
  8.0 0.0 all-gather.3.cloned.1.call-start
  8.0 0.7 all-gather.3.cloned.1.call-update
  8.7 0.0 reduce-scatter.2.cloned.1.call-start
  8.8 3.5 %reshape.152 = bf16[1,64,32,240]{3,2,1,0:T(8,128)(2,1)S(1)} reshape(bf16[1,1,64,7680]{3,2,1,0:T(8,128)(2,1)} %param.7) | data formatting | bytes 1966080 | tf_op jit(solution)/shard_map/reshape | solution.py:67
  12.3 0.6 copy.29
  12.9 47.7 %all_to_all.52 = bf16[1,64,32,240]{3,1,0,2:T(8,128)(2,1)S(1)} all-to-all(bf16[1,64,32,240]{3,1,0,2:T(8,128)(2,1)S(1)} %copy.29), channel_id=1, replica_groups=mesh['grp'=2,'section'=2,'seq'=4,'fsdp'=2] {'seq'}, dimensions={2} | all-to-all | bytes 1966080 | tf_op jit(solution)/shard_map/all_to_all | solution.py:69
  60.6 0.6 copy.46
  61.2 0.1 copy.31
  61.2 0.4 fusion.30
  61.7 0.3 copy.42
  62.0 0.3 copy.43
  62.3 0.3 copy.44
  62.7 2.2 %fusion.32 = (f32[8,256]{1,0:T(8,128)S(1)}, f32[8,256,256]{1,2,0:T(8,128)}) fusion(bf16[1,256,8,80]{1,3,2,0:T(8,128)(2,1)S(1)} %copy.44, bf16[1,256,8,80]{1,3,2,0:T(8,128)(2,1)S(1)} %copy.43), kind=kOutput, calls=%fused_computation.36 | convolution fusion | flops 85459200 | bytes 2760704 | tf_op jit(solution)/shard_map/while/body/eval_jaxpr/sub | solution.py:52
  64.8 1.9 %convolution_convert_fusion = bf16[8,256,80]{1,2,0:T(8,128)(2,1)S(1)} fusion(f32[8,256,256]{1,2,0:T(8,128)} %get-tuple-element.26, f32[8,256]{1,0:T(8,128)S(1)} %get-tuple-element.25, bf16[1,256,8,80]{1,3,2,0:T(8,128)(2,1)S(1)} %copy.42), kind=kOutput, calls=%fused_computation.10 | convolution fusion | flops 85098496 | bytes 2760704 | tf_op jit(solution)/shard_map/while/body/eval_jaxpr/nhqk,nkhe->nqhe/dot_general | solution.py:55
  66.7 0.6 copy.36
  67.3 0.5 broadcast.88
  67.9 2.6 %reduce.14 = bf16[256,640]{1,0:T(8,128)(2,1)S(1)} reduce(bf16[256,1,640]{2,1,0:T(2,128)(2,1)S(1)} %bitcast.71, bf16[]{:T(256)} %broadcast.88), dimensions={1}, to_apply=%bitcast.59.reduce_sub_computation | reduce | bytes 655362
  70.5 0.1 reshape.168
  70.6 22.7 %all_to_all.53 = bf16[4,2,20480]{2,1,0:T(2,128)(2,1)S(1)} all-to-all(bf16[4,2,20480]{2,1,0:T(2,128)(2,1)S(1)} %reshape.168), channel_id=1, replica_groups=mesh['grp'=2,'section'=2,'seq'=4,'fsdp'=2] {'seq'}, dimensions={0} | all-to-all | bytes 655360 | tf_op jit(solution)/shard_map/all_to_all | solution.py:68
  93.2 0.3 reshape.169
  93.6 0.3 copy.37
  93.9 0.2 all_to_all.45
  94.1 8.1 %all_to_all.54 = bf16[64,2,1280]{2,0,1:T(8,128)(2,1)S(1)} all-to-all(bf16[64,2,1280]{2,0,1:T(8,128)(2,1)S(1)} %copy.38), channel_id=1, replica_groups=mesh['grp'=2,'section'=2,'seq'=4,'fsdp'=2] {'fsdp'}, dimensions={1} | all-to-all | bytes 655360 | tf_op jit(solution)/shard_map/all_to_all | solution.py:85
  102.2 0.0 copy-start.4
  102.2 0.0 copy-start.2
  102.2 4.7 %fusion.5 = bf16[128,2560]{1,0:T(8,128)(2,1)} fusion(bf16[128,1280]{1,0:T(8,128)(2,1)S(1)} %bitcast.73, bf16[1,1280,2560]{2,1,0:T(8,128)(2,1)} %param.9), kind=kOutput, calls=%fused_computation.5 | convolution fusion | flops 839188480 | bytes 7536640 | tf_op jit(solution)/shard_map/dot_general | solution.py:87
  106.9 0.0 reduce-scatter.2.cloned.1.call-update
  106.9 0.0 copy-done.4
  107.0 0.6 fusion.31
  108.8 0.1 sine_convert_fusion
  108.9 0.0 copy-done.2
  108.9 31.4 %all-gather = bf16[8,320,64]{1,2,0:T(8,128)(2,1)S(1)} all-gather(bf16[1,320,64]{1,2,0:T(8,128)(2,1)S(1)} %copy-done.2), channel_id=2, replica_groups=mesh['grp'=2,'section'=2,'seq'=4,'fsdp'=2] {'seq','fsdp'}, dimensions={0}, use_global_device_ids=true | all-gather | bytes 368640 | tf_op jit(solution)/shard_map/all_gather | solution.py:78
  140.4 0.2 copy.39
  140.6 0.3 squeeze_reshape.3
  140.9 0.0 copy-start
  141.0 0.0 all-gather.3.cloned.1.call-done
  141.0 3.2 %fusion.3 = f32[1,7680]{1,0:T(1,128)S(1)} fusion(bf16[256,1]{0,1:T(2,128)(2,1)S(1)} %reshape.162, bf16[1,256,7680]{1,2,0:T(8,128)(2,1)} %all-gather.3.cloned.1.call-done), kind=kOutput, calls=%fused_computation.3 | convolution fusion | flops 3932160 | bytes 3963392 | tf_op jit(solution)/shard_map/dot_general | solution.py:81
  144.2 0.0 copy-start.3
  144.2 0.1 slice_reduce_fusion.1
  144.3 0.0 reduce-scatter.2.cloned.1.call-done
  144.4 0.0 copy-done
  144.4 1.2 fusion.10
  145.6 1.2 multiply_reduce_fusion.1
  146.8 1.3 fusion.15
  148.1 0.1 reshape.156
  148.2 0.0 copy-start.1
  148.2 0.0 copy-done.3
  148.2 0.1 collective-permute-start
  148.3 1.2 collective-permute-done
  149.5 0.6 copy.48
  150.1 0.0 copy-done.1
  (7 shorter events, 0.1 us)
Async XLA Ops:
  8.0 133.0 %all-gather.3.cloned.1.call-start = ((), (), s32[]{:S(2)}) async-start(), calls=%async_computation.4 | async-start | bytes 4423680 | tf_op jit(solution)/shard_map/all_gather | solution.py:77
  8.7 135.6 %reduce-scatter.2.cloned.1.call-start = ((), (), s32[]{:S(2)}) async-start(), calls=%async_computation.5 | async-start | bytes 983040 | tf_op jit(solution)/shard_map/reduce_scatter | solution.py:86
  102.2 4.8 %copy-start.4 = (s32[1,1,2]{2,1,0:T(1,128)S(1)}, s32[1,1,2]{2,1,0:T(1,128)}, u32[]{:S(2)}) copy-start(s32[1,1,2]{2,1,0:T(1,128)} %param.13) | copy-start | bytes 28
  102.2 6.7 %copy-start.2 = (bf16[1,320,64]{1,2,0:T(8,128)(2,1)S(1)}, bf16[1,320,64]{1,2,0:T(8,128)(2,1)}, u32[]{:S(2)}) copy-start(bf16[1,320,64]{1,2,0:T(8,128)(2,1)} %param.11) | copy-start | bytes 122884
  140.9 3.5 %copy-start = (bf16[1,1,64,2560]{3,2,1,0:T(8,128)(2,1)S(1)}, bf16[1,1,64,2560]{3,2,1,0:T(8,128)(2,1)}, u32[]{:S(2)}) copy-start(bf16[1,1,64,2560]{3,2,1,0:T(8,128)(2,1)} %param.8) | copy-start | bytes 983044
  144.2 4.0 %copy-start.3 = (f32[1,1,32,128]{3,2,1,0:T(8,128)S(1)}, f32[1,1,32,128]{3,2,1,0:T(8,128)}, u32[]{:S(2)}) copy-start(f32[1,1,32,128]{3,2,1,0:T(8,128)} %param.12) | copy-start | bytes 49156
  148.2 1.9 %copy-start.1 = (f32[1,1,32,128]{3,2,1,0:T(8,128)}, f32[1,1,32,128]{3,2,1,0:T(8,128)S(1)}, u32[]{:S(2)}) copy-start(f32[1,1,32,128]{3,2,1,0:T(8,128)S(1)} %reshape.156) | copy-start | bytes 49156
  148.2 1.2 collective-permute-start
Sparse Core Ops, SparseCore 0:
  11.0 94.3 all-gather.2
Sparse Core Ops, SparseCore 1:
  107.0 17.1 reduce-scatter.1
